TPU v7x, 32 devices: a whole 2x2x4 slice. The times are simulated.
32 devices in a mesh: path: 4 (over z), trade: 8 (over y, x, core).
Axes of the slice: x: 2, y: 2, z: 4, core: 2. Of those that a mesh axis runs over, the one named last changes fastest.
Arguments:
- factors: bfloat16 [32, 8, 512], P(None, None, 'path'), may hold values from -5 to 5
- loadings: bfloat16 [32, 8, 32768], P(None, None, 'trade'), may hold values from -0.5 to 0.5
- notional: float32 [32768], P('trade'), may hold values from -1 to 1
- strike: float32 [32768], P('trade'), may hold values from 0.5 to 1.5
- date_weight: float32 [32], replicated, may hold values from 0.3 to 3
- loss_spanning: float32 [128], replicated, may hold values from 0.2 to 0.9
- loss_local: float32 [1024], P('trade'), may hold values from 0.2 to 0.9
- trade_slot: int32 [32768], P('trade'), may hold values from 0 to 255
- span_list: int32 [1024], P('trade'), may hold values from 0 to 127, as said below
Outputs:
- loading_grad: float32 [32, 8, 32768], P('path', None, 'trade')
- factor_grad: float32 [32, 8, 512], P('trade', None, 'path')
Inputs may be any that keep to these rules, and one draw needn't show every extreme that they name: `trade_slot`: slot s < 128 of a trade shard holds that shard's spanning set from span_list; slot 128 + i holds the shard's i-th local set. `span_list`: the 128 entries of one trade shard are distinct spanning set ids.
All inputs are finite; a program needn't handle non-finite values.
Results may differ from a plain program's by a relative error of at most 0.0021.
Values may be sent and summed in bfloat16 or wider, within the bound.
A program may use at most 64 MiB of HBM per device.

v0:
```python
import math

import jax
import jax.numpy as jnp
from jax import lax
from jax.sharding import PartitionSpec as P

smoothing = 0.5


def price(factor_block, loading_block):
    exponent = jnp.einsum(
        "bfp,bfk->bpk", factor_block, loading_block, preferred_element_type=jnp.float32
    )
    return jnp.exp(exponent)


def on_device(
    factors,
    loadings,
    notional,
    strike,
    date_weight,
    loss_spanning,
    loss_local,
    trade_slot,
    span_list,
):
    path_total = lax.axis_size("path") * factors.shape[2]
    factor_here = lax.all_to_all(factors, "path", split_axis=0, concat_axis=2, tiled=True)
    dates_here = factor_here.shape[0]
    first_date = lax.axis_index("path") * dates_here
    loading_here = lax.dynamic_slice_in_dim(loadings, first_date, dates_here, 0)
    weight_here = lax.dynamic_slice_in_dim(date_weight, first_date, dates_here, 0)
    date_count = factor_here.shape[0]
    factor_count = factor_here.shape[1]
    path_local = factor_here.shape[2]
    trade_local = loading_here.shape[2]
    span_local = span_list.shape[0]
    span_count = loss_spanning.shape[0]
    slot_count = span_local + loss_local.shape[0]
    dates_per_step = math.gcd(date_count, max(1, 512 // path_local))
    block_count = date_count // dates_per_step
    slot_table = (trade_slot[:, None] == jnp.arange(slot_count, dtype=jnp.int32)[None, :]).astype(
        jnp.bfloat16
    )
    set_match = span_list[:, None] == jnp.arange(span_count, dtype=jnp.int32)[None, :]
    set_table = set_match.astype(jnp.float32)
    set_select = set_match.astype(jnp.bfloat16)
    factor_blocks = factor_here.reshape(block_count, dates_per_step, factor_count, path_local)
    loading_blocks = loading_here.reshape(block_count, dates_per_step, factor_count, trade_local)
    weight_blocks = weight_here.reshape(block_count, dates_per_step)

    def forward(operands):
        factor_block, loading_block, weight_block = operands
        growth = price(factor_block, loading_block)
        values = (notional * (growth - strike)).astype(jnp.bfloat16)
        partial_sums = jnp.einsum(
            "bpk,ks->bps", values, slot_table, preferred_element_type=jnp.float32
        )
        span_part = jnp.einsum(
            "bps,sn->bpn",
            partial_sums[:, :, :span_local],
            set_table,
            precision=lax.Precision.HIGHEST,
            preferred_element_type=jnp.float32,
        )
        local_weight = (
            weight_block[:, None, None]
            * loss_local
            * jax.nn.sigmoid(partial_sums[:, :, span_local:] / smoothing)
        ).astype(jnp.bfloat16)
        return (span_part, local_weight)

    span_parts, local_weights = lax.map(forward, (factor_blocks, loading_blocks, weight_blocks))
    span_parts = span_parts.reshape(date_count, path_local, span_count)
    span_total = lax.psum(span_parts, "trade")
    span_weight = (
        weight_here[:, None, None] * loss_spanning * jax.nn.sigmoid(span_total / smoothing)
    ).astype(jnp.bfloat16)
    span_blocks = span_weight.reshape(block_count, dates_per_step, path_local, span_count)

    def adjoint(operands):
        factor_block, loading_block, span_block, local_block = operands
        growth = price(factor_block, loading_block)
        span_slots = jnp.einsum(
            "bpn,sn->bps", span_block, set_select, preferred_element_type=jnp.float32
        ).astype(jnp.bfloat16)
        slot_weight = jnp.concatenate([span_slots, local_block], axis=2)
        trade_weight = jnp.einsum(
            "bps,ks->bpk", slot_weight, slot_table, preferred_element_type=jnp.float32
        )
        sensitivity = (trade_weight * notional * growth).astype(jnp.bfloat16)
        loading_term = jnp.einsum(
            "bfp,bpk->bfk", factor_block, sensitivity, preferred_element_type=jnp.float32
        )
        factor_term = jnp.einsum(
            "bfk,bpk->bfp", loading_block, sensitivity, preferred_element_type=jnp.float32
        )
        return (loading_term, factor_term)

    loading_terms, factor_terms = lax.map(
        adjoint, (factor_blocks, loading_blocks, span_blocks, local_weights)
    )
    loading_terms = loading_terms.reshape(date_count, factor_count, trade_local)
    factor_terms = factor_terms.reshape(date_count, factor_count, path_local)
    loading_grad = loading_terms / path_total
    regrouped = lax.all_to_all(factor_terms, "path", split_axis=2, concat_axis=0, tiled=True)
    factor_grad = lax.psum_scatter(regrouped, "trade", scatter_dimension=0, tiled=True)
    return (loading_grad, factor_grad)


def solution(mesh):
    return jax.shard_map(
        on_device,
        mesh=mesh,
        in_specs=(
            P(None, None, "path"),
            P(None, None, "trade"),
            P("trade"),
            P("trade"),
            P(),
            P(),
            P("trade"),
            P("trade"),
            P("trade"),
        ),
        out_specs=(P("path", None, "trade"), P("trade", None, "path")),
        check_vma=False,
    )
```

profile of v0, /device:TPU:7, one launch (start us, length us, event | category | flops | bytes accessed | tf_op | source)
XLA Modules:
  0.0 281.7 jit_solution(14998099556894631179)
XLA Ops:
  7.2 4.7 %all-to-all-start = ((bf16[32,8,128]{2,1,0:T(8,128)(2,1)}), bf16[32,8,128]{2,1,0:T(8,128)(2,1)S(1)}, u32[]{:S(2)}, u32[]{:S(2)}) async-start(bf16[32,8,128]{2,1,0:T(8,128)(2,1)} %param.13), calls=%async_computation | async-start | bytes 131072 | tf_op jit(solution)/shard_map/all_to_all | solution.py:30
  12.7 3.8 %all-to-all-done = bf16[32,8,128]{2,1,0:T(8,128)(2,1)S(1)} async-done(((bf16[32,8,128]{2,1,0:T(8,128)(2,1)}), bf16[32,8,128]{2,1,0:T(8,128)(2,1)S(1)}, u32[]{:S(2)}, u32[]{:S(2)}) %all-to-all-start) | async-done | bytes 65568 | tf_op jit(solution)/shard_map/all_to_all | solution.py:30
  16.5 50.6 %while.26 = (s32[]{:T(128)}, f32[8,1,512,128]{3,2,1,0:T(8,128)}, bf16[8,1,512,128]{3,2,1,0:T(8,128)(2,1)}, f32[4096]{0:T(1024)}, bf16[8,1,8,512]{3,2,1,0:T(8,128...) while((s32[]{:T(128)}, f32[8,1,512,128]{3,2,1,0:T(8,128)}, ...), condition=%wide.region_1.2_spmd.clone, body=%wide.region_0.1_spmd.clone.sunk | while | flops 1216774272 | bytes 1573053 | solution.py:75
  16.6 3.3 %fusion.88 = f32[1,512,256]{2,1,0:T(8,128)S(1)} fusion(s32[4096]{0:T(1024)} %get-tuple-element.392, f32[4096]{0:T(1024)} %get-tuple-element.389, f32[4096]{0:T(1024)} %get-tuple-element.386, bf16[8,1,8,4096]{3,2,1,0:T(8,128)(2,1)S(1)} %get-tuple-element.388, s32[]{:T(128)} %get-tuple-element.371, bf16[8,1,8,512]{3,2,1,0:T(8,128)(2,1)S(1)} %get-tuple-element.387), kind=kOutput, calls=%fused_computation.9.clone.1 | convolution fusion | flops 1115684864 | bytes 648192 | tf_op jit(solution)/shard_map/while/body/eval_jaxpr/bpk,ks->bps/dot_general | solution.py:58
  22.9 3.3 %fusion.88 = f32[1,512,256]{2,1,0:T(8,128)S(1)} fusion(s32[4096]{0:T(1024)} %get-tuple-element.392, f32[4096]{0:T(1024)} %get-tuple-element.389, f32[4096]{0:T(1024)} %get-tuple-element.386, bf16[8,1,8,4096]{3,2,1,0:T(8,128)(2,1)S(1)} %get-tuple-element.388, s32[]{:T(128)} %get-tuple-element.371, bf16[8,1,8,512]{3,2,1,0:T(8,128)(2,1)S(1)} %get-tuple-element.387), kind=kOutput, calls=%fused_computation.9.clone.1 | convolution fusion | flops 1115684864 | bytes 648192 | tf_op jit(solution)/shard_map/while/body/eval_jaxpr/bpk,ks->bps/dot_general | solution.py:58
  29.2 3.3 %fusion.88 = f32[1,512,256]{2,1,0:T(8,128)S(1)} fusion(s32[4096]{0:T(1024)} %get-tuple-element.392, f32[4096]{0:T(1024)} %get-tuple-element.389, f32[4096]{0:T(1024)} %get-tuple-element.386, bf16[8,1,8,4096]{3,2,1,0:T(8,128)(2,1)S(1)} %get-tuple-element.388, s32[]{:T(128)} %get-tuple-element.371, bf16[8,1,8,512]{3,2,1,0:T(8,128)(2,1)S(1)} %get-tuple-element.387), kind=kOutput, calls=%fused_computation.9.clone.1 | convolution fusion | flops 1115684864 | bytes 648192 | tf_op jit(solution)/shard_map/while/body/eval_jaxpr/bpk,ks->bps/dot_general | solution.py:58
  35.5 3.3 %fusion.88 = f32[1,512,256]{2,1,0:T(8,128)S(1)} fusion(s32[4096]{0:T(1024)} %get-tuple-element.392, f32[4096]{0:T(1024)} %get-tuple-element.389, f32[4096]{0:T(1024)} %get-tuple-element.386, bf16[8,1,8,4096]{3,2,1,0:T(8,128)(2,1)S(1)} %get-tuple-element.388, s32[]{:T(128)} %get-tuple-element.371, bf16[8,1,8,512]{3,2,1,0:T(8,128)(2,1)S(1)} %get-tuple-element.387), kind=kOutput, calls=%fused_computation.9.clone.1 | convolution fusion | flops 1115684864 | bytes 648192 | tf_op jit(solution)/shard_map/while/body/eval_jaxpr/bpk,ks->bps/dot_general | solution.py:58
  41.8 3.3 %fusion.88 = f32[1,512,256]{2,1,0:T(8,128)S(1)} fusion(s32[4096]{0:T(1024)} %get-tuple-element.392, f32[4096]{0:T(1024)} %get-tuple-element.389, f32[4096]{0:T(1024)} %get-tuple-element.386, bf16[8,1,8,4096]{3,2,1,0:T(8,128)(2,1)S(1)} %get-tuple-element.388, s32[]{:T(128)} %get-tuple-element.371, bf16[8,1,8,512]{3,2,1,0:T(8,128)(2,1)S(1)} %get-tuple-element.387), kind=kOutput, calls=%fused_computation.9.clone.1 | convolution fusion | flops 1115684864 | bytes 648192 | tf_op jit(solution)/shard_map/while/body/eval_jaxpr/bpk,ks->bps/dot_general | solution.py:58
  48.1 3.3 %fusion.88 = f32[1,512,256]{2,1,0:T(8,128)S(1)} fusion(s32[4096]{0:T(1024)} %get-tuple-element.392, f32[4096]{0:T(1024)} %get-tuple-element.389, f32[4096]{0:T(1024)} %get-tuple-element.386, bf16[8,1,8,4096]{3,2,1,0:T(8,128)(2,1)S(1)} %get-tuple-element.388, s32[]{:T(128)} %get-tuple-element.371, bf16[8,1,8,512]{3,2,1,0:T(8,128)(2,1)S(1)} %get-tuple-element.387), kind=kOutput, calls=%fused_computation.9.clone.1 | convolution fusion | flops 1115684864 | bytes 648192 | tf_op jit(solution)/shard_map/while/body/eval_jaxpr/bpk,ks->bps/dot_general | solution.py:58
  54.4 3.3 %fusion.88 = f32[1,512,256]{2,1,0:T(8,128)S(1)} fusion(s32[4096]{0:T(1024)} %get-tuple-element.392, f32[4096]{0:T(1024)} %get-tuple-element.389, f32[4096]{0:T(1024)} %get-tuple-element.386, bf16[8,1,8,4096]{3,2,1,0:T(8,128)(2,1)S(1)} %get-tuple-element.388, s32[]{:T(128)} %get-tuple-element.371, bf16[8,1,8,512]{3,2,1,0:T(8,128)(2,1)S(1)} %get-tuple-element.387), kind=kOutput, calls=%fused_computation.9.clone.1 | convolution fusion | flops 1115684864 | bytes 648192 | tf_op jit(solution)/shard_map/while/body/eval_jaxpr/bpk,ks->bps/dot_general | solution.py:58
  60.8 3.3 %fusion.88 = f32[1,512,256]{2,1,0:T(8,128)S(1)} fusion(s32[4096]{0:T(1024)} %get-tuple-element.392, f32[4096]{0:T(1024)} %get-tuple-element.389, f32[4096]{0:T(1024)} %get-tuple-element.386, bf16[8,1,8,4096]{3,2,1,0:T(8,128)(2,1)S(1)} %get-tuple-element.388, s32[]{:T(128)} %get-tuple-element.371, bf16[8,1,8,512]{3,2,1,0:T(8,128)(2,1)S(1)} %get-tuple-element.387), kind=kOutput, calls=%fused_computation.9.clone.1 | convolution fusion | flops 1115684864 | bytes 648192 | tf_op jit(solution)/shard_map/while/body/eval_jaxpr/bpk,ks->bps/dot_general | solution.py:58
  67.9 59.0 %all-reduce.2.cloned.1.call-done = f32[8,512,128]{2,1,0:T(8,128)} async-done(((f32[8,512,128]{2,1,0:T(8,128)}), f32[8,512,128]{2,1,0:T(8,128)}) %all-reduce.2.cloned.1.call-update) | async-done | bytes 2097168 | tf_op jit(solution)/shard_map/psum | solution.py:77
  129.1 88.6 %while.27 = (s32[]{:T(128)}, f32[8,1,8,4096]{3,2,1,0:T(8,128)}, f32[8,1,8,512]{3,2,1,0:T(8,128)}, bf16[8,1,8,512]{3,2,1,0:T(8,128)(2,1)S(1)}, bf16[8,1,512,128]{...) while((s32[]{:T(128)}, f32[8,1,8,4096]{3,2,1,0:T(8,128)}, ...), condition=%wide.region_4.5_spmd.clone, body=%wide.region_3.4_spmd.clone.sunk | while | flops 1200193536 | bytes 31266512 | solution.py:102
  131.0 2.6 fusion.100
  137.6 2.6 fusion.102
  142.1 2.6 fusion.100
  153.2 2.6 fusion.100
  164.2 2.6 fusion.100
  170.8 2.6 fusion.102
  175.3 2.6 fusion.100
  186.4 2.6 fusion.100
  192.9 2.6 fusion.102
  197.4 2.6 fusion.100
  204.0 2.6 fusion.102
  208.5 2.6 fusion.100
  215.1 2.6 fusion.102
  217.7 2.9 %copy.18 = f32[8,1,8,512]{2,0,3,1:T(8,128)} copy(f32[8,1,8,512]{3,2,1,0:T(8,128)} %get-tuple-element.445) | data formatting | bytes 262144 | tf_op jit(solution)/shard_map/while | solution.py:102
  220.5 3.1 %bitcast_bitcast_fusion = f32[512,8,8]{2,1,0:T(8,128)} fusion(f32[8,1,8,512]{2,0,3,1:T(8,128)} %copy.18), kind=kLoop, calls=%fused_computation.71 | loop fusion | bytes 262144
  223.6 2.7 reshape.144
  226.3 9.0 %all_to_all.33 = f32[4,1,8192]{2,1,0:T(1,128)S(1)} all-to-all(f32[4,1,8192]{2,1,0:T(1,128)S(1)} %reshape.144), channel_id=1, replica_groups=mesh['path'=4,'trade'=8] {'path'}, dimensions={0} | all-to-all | bytes 262144 | tf_op jit(solution)/shard_map/all_to_all | solution.py:108
  239.3 2.8 copy.19
  244.4 30.5 %reduce-scatter.2.cloned.1.call-done = f32[4,8,128]{2,1,0:T(8,128)} async-done(((f32[32,8,128]{2,1,0:T(8,128)}), f32[4,8,128]{2,1,0:T(8,128)}) %reduce-scatter.2.cloned.1.call-update) | async-done | bytes 16400 | tf_op jit(solution)/shard_map/reduce_scatter | solution.py:109
  (185 shorter events, 88.0 us)
Async XLA Ops:
  7.2 4.8 %copy-start = (bf16[32,8,4096]{2,1,0:T(8,128)(2,1)S(1)}, bf16[32,8,4096]{2,1,0:T(8,128)(2,1)}, u32[]{:S(2)}) copy-start(bf16[32,8,4096]{2,1,0:T(8,128)(2,1)} %param.14) | copy-start | bytes 6291460
  7.2 9.3 %all-to-all-start = ((bf16[32,8,128]{2,1,0:T(8,128)(2,1)}), bf16[32,8,128]{2,1,0:T(8,128)(2,1)S(1)}, u32[]{:S(2)}, u32[]{:S(2)}) async-start(bf16[32,8,128]{2,1,0:T(8,128)(2,1)} %param.13), calls=%async_computation | async-start | bytes 131072 | tf_op jit(solution)/shard_map/all_to_all | solution.py:30
  11.9 115.0 %all-reduce.2.cloned.1.call-start = ((), (), s32[]{:S(2)}) async-start(), calls=%async_computation.3 | async-start | bytes 4194304 | tf_op jit(solution)/shard_map/psum | solution.py:77
  16.5 50.7 %copy-start.10 = (f32[32]{0:T(128)S(1)}, f32[32]{0:T(128)}, u32[]{:S(2)}) copy-start(f32[32]{0:T(128)} %param.17) | copy-start | bytes 388
  16.5 50.7 %copy-start.8 = (f32[128]{0:T(128)S(1)}, f32[128]{0:T(128)}, u32[]{:S(2)}) copy-start(f32[128]{0:T(128)} %param.18) | copy-start | bytes 1540
  16.6 3.9 %copy-start.9 = (f32[128]{0:T(128)S(1)}, f32[128]{0:T(128)}, u32[]{:S(2)}) copy-start(f32[128]{0:T(128)} %get-tuple-element.391) | copy-start | bytes 1540 | tf_op jit(solution)/shard_map/while
  16.6 5.2 %copy-start.5 = (s32[128]{0:T(128)S(1)}, s32[128]{0:T(128)}, u32[]{:S(2)}) copy-start(s32[128]{0:T(128)} %get-tuple-element.393) | copy-start | bytes 1540 | tf_op jit(solution)/shard_map/while
  22.9 3.9 %copy-start.9 = (f32[128]{0:T(128)S(1)}, f32[128]{0:T(128)}, u32[]{:S(2)}) copy-start(f32[128]{0:T(128)} %get-tuple-element.391) | copy-start | bytes 1540 | tf_op jit(solution)/shard_map/while
  22.9 5.2 %copy-start.5 = (s32[128]{0:T(128)S(1)}, s32[128]{0:T(128)}, u32[]{:S(2)}) copy-start(s32[128]{0:T(128)} %get-tuple-element.393) | copy-start | bytes 1540 | tf_op jit(solution)/shard_map/while
  29.2 3.9 %copy-start.9 = (f32[128]{0:T(128)S(1)}, f32[128]{0:T(128)}, u32[]{:S(2)}) copy-start(f32[128]{0:T(128)} %get-tuple-element.391) | copy-start | bytes 1540 | tf_op jit(solution)/shard_map/while
  29.2 5.2 %copy-start.5 = (s32[128]{0:T(128)S(1)}, s32[128]{0:T(128)}, u32[]{:S(2)}) copy-start(s32[128]{0:T(128)} %get-tuple-element.393) | copy-start | bytes 1540 | tf_op jit(solution)/shard_map/while
  35.5 3.9 %copy-start.9 = (f32[128]{0:T(128)S(1)}, f32[128]{0:T(128)}, u32[]{:S(2)}) copy-start(f32[128]{0:T(128)} %get-tuple-element.391) | copy-start | bytes 1540 | tf_op jit(solution)/shard_map/while
  35.5 5.1 %copy-start.5 = (s32[128]{0:T(128)S(1)}, s32[128]{0:T(128)}, u32[]{:S(2)}) copy-start(s32[128]{0:T(128)} %get-tuple-element.393) | copy-start | bytes 1540 | tf_op jit(solution)/shard_map/while
  41.8 3.9 %copy-start.9 = (f32[128]{0:T(128)S(1)}, f32[128]{0:T(128)}, u32[]{:S(2)}) copy-start(f32[128]{0:T(128)} %get-tuple-element.391) | copy-start | bytes 1540 | tf_op jit(solution)/shard_map/while
  41.8 5.2 %copy-start.5 = (s32[128]{0:T(128)S(1)}, s32[128]{0:T(128)}, u32[]{:S(2)}) copy-start(s32[128]{0:T(128)} %get-tuple-element.393) | copy-start | bytes 1540 | tf_op jit(solution)/shard_map/while
  48.1 3.9 %copy-start.9 = (f32[128]{0:T(128)S(1)}, f32[128]{0:T(128)}, u32[]{:S(2)}) copy-start(f32[128]{0:T(128)} %get-tuple-element.391) | copy-start | bytes 1540 | tf_op jit(solution)/shard_map/while
  48.1 5.2 %copy-start.5 = (s32[128]{0:T(128)S(1)}, s32[128]{0:T(128)}, u32[]{:S(2)}) copy-start(s32[128]{0:T(128)} %get-tuple-element.393) | copy-start | bytes 1540 | tf_op jit(solution)/shard_map/while
  54.4 3.9 %copy-start.9 = (f32[128]{0:T(128)S(1)}, f32[128]{0:T(128)}, u32[]{:S(2)}) copy-start(f32[128]{0:T(128)} %get-tuple-element.391) | copy-start | bytes 1540 | tf_op jit(solution)/shard_map/while
  54.4 5.2 %copy-start.5 = (s32[128]{0:T(128)S(1)}, s32[128]{0:T(128)}, u32[]{:S(2)}) copy-start(s32[128]{0:T(128)} %get-tuple-element.393) | copy-start | bytes 1540 | tf_op jit(solution)/shard_map/while
  60.8 3.9 %copy-start.9 = (f32[128]{0:T(128)S(1)}, f32[128]{0:T(128)}, u32[]{:S(2)}) copy-start(f32[128]{0:T(128)} %get-tuple-element.391) | copy-start | bytes 1540 | tf_op jit(solution)/shard_map/while
  60.8 5.2 %copy-start.5 = (s32[128]{0:T(128)S(1)}, s32[128]{0:T(128)}, u32[]{:S(2)}) copy-start(s32[128]{0:T(128)} %get-tuple-element.393) | copy-start | bytes 1540 | tf_op jit(solution)/shard_map/while
  67.1 62.0 %copy-start.2 = (f32[4096]{0:T(1024)S(1)}, f32[4096]{0:T(1024)}, u32[]{:S(2)}) copy-start(f32[4096]{0:T(1024)} %get-tuple-element.436) | copy-start | bytes 49156
  67.1 62.0 %copy-start.6 = (s32[128]{0:T(128)S(1)}, s32[128]{0:T(128)}, u32[]{:S(2)}) copy-start(s32[128]{0:T(128)} %get-tuple-element.442) | copy-start | bytes 1540
  67.1 207.7 %reduce-scatter.2.cloned.1.call-start = ((), (), s32[]{:S(2)}) async-start(), calls=%async_computation.4 | async-start | bytes 147456 | tf_op jit(solution)/shard_map/reduce_scatter | solution.py:109
  136.2 4.0 %copy-start.7 = (s32[128]{0:T(128)S(1)}, s32[128]{0:T(128)}, u32[]{:S(2)}) copy-start(s32[128]{0:T(128)} %get-tuple-element.454) | copy-start | bytes 1540 | tf_op jit(solution)/shard_map/while
  147.3 4.0 %copy-start.7 = (s32[128]{0:T(128)S(1)}, s32[128]{0:T(128)}, u32[]{:S(2)}) copy-start(s32[128]{0:T(128)} %get-tuple-element.454) | copy-start | bytes 1540 | tf_op jit(solution)/shard_map/while
  158.4 4.0 %copy-start.7 = (s32[128]{0:T(128)S(1)}, s32[128]{0:T(128)}, u32[]{:S(2)}) copy-start(s32[128]{0:T(128)} %get-tuple-element.454) | copy-start | bytes 1540 | tf_op jit(solution)/shard_map/while
  169.4 4.0 %copy-start.7 = (s32[128]{0:T(128)S(1)}, s32[128]{0:T(128)}, u32[]{:S(2)}) copy-start(s32[128]{0:T(128)} %get-tuple-element.454) | copy-start | bytes 1540 | tf_op jit(solution)/shard_map/while
  180.5 4.0 %copy-start.7 = (s32[128]{0:T(128)S(1)}, s32[128]{0:T(128)}, u32[]{:S(2)}) copy-start(s32[128]{0:T(128)} %get-tuple-element.454) | copy-start | bytes 1540 | tf_op jit(solution)/shard_map/while
  191.6 4.0 %copy-start.7 = (s32[128]{0:T(128)S(1)}, s32[128]{0:T(128)}, u32[]{:S(2)}) copy-start(s32[128]{0:T(128)} %get-tuple-element.454) | copy-start | bytes 1540 | tf_op jit(solution)/shard_map/while
  202.6 4.0 %copy-start.7 = (s32[128]{0:T(128)S(1)}, s32[128]{0:T(128)}, u32[]{:S(2)}) copy-start(s32[128]{0:T(128)} %get-tuple-element.454) | copy-start | bytes 1540 | tf_op jit(solution)/shard_map/while
  213.7 4.0 %copy-start.7 = (s32[128]{0:T(128)S(1)}, s32[128]{0:T(128)}, u32[]{:S(2)}) copy-start(s32[128]{0:T(128)} %get-tuple-element.454) | copy-start | bytes 1540 | tf_op jit(solution)/shard_map/while
  (17 other events, 26.3 us)
Sparse Core Ops, SparseCore 0:
  67.3 59.6 all-reduce.1
  242.2 32.6 reduce-scatter.1
where the time goes:
time: 287 us; the launch traced here: 282 us
  matrix products  110 us (38%)
  waiting for transfers between devices  93.3 us (33%)
  local copies, waits for them, and re-layouts  33.8 us (12%)
  other arithmetic  15.8 us (6%)
  between operations  14.1 us (5%)
  blocking collectives  8.99 us (3%)
  starting transfers between devices  4.78 us (2%)
    psum x1, waiting for transfers between devices, on_device(): span_total = lax.psum(span_parts, 'trade')  59 us
    reduce_scatter x1, waiting for transfers between devices, on_device(): lax.psum_scatter(regrouped, 'trade', scatter_dimension=0, tiled=True)  30.5 us
    dot_general x8, matrix products, forward(): jnp.einsum('bpk,ks->bps', values, slot_table, preferred_element_type=jnp....  26.4 us
    dot_general x8, matrix products, adjoint(): jnp.einsum('bps,ks->bpk', slot_weight, slot_table, preferred_element_type...  21.1 us
    dot_general x8, matrix products, adjoint(): jnp.einsum('bfk,bpk->bfp', loading_block, sensitivity, preferred_element_...  21.1 us
    dot_general x8, matrix products, price(): jnp.einsum('bfp,bfk->bpk', factor_block, loading_block, preferred_element...  20.3 us
    dot_general x8, matrix products, adjoint(): jnp.einsum('bfp,bpk->bfk', factor_block, sensitivity, preferred_element_t...  10.5 us
    dot_general x8, matrix products, forward(): jnp.einsum('bps,sn->bpn', partial_sums[:, :, :span_local], set_table, pre...  9.18 us
  transfers between devices with their start and end apart: 3, of which 3 were waited for; matrix products, arithmetic and copies ran while one was open for 1% of the time, Pallas kernels for 0%

commit v1 on v0

v1 whole, which is shorter than its diff:
```python
import functools
import math

import jax
import jax.numpy as jnp
from jax import lax
from jax.experimental import pallas as pl
from jax.experimental.pallas import tpu as pltpu
from jax.sharding import PartitionSpec as P

smoothing = 0.5
MESH = pl.DeviceIdType.MESH
chunk = 512
bf16 = jnp.bfloat16
f32 = jnp.float32


def dot(a, b):
    return jnp.dot(a, b, preferred_element_type=f32)


def kernel(
    n_path,
    n_trade,
    factors_ref,
    loadings_ref,
    notional_ref,
    strike_ref,
    date_weight_ref,
    loss_span_ref,
    loss_local_ref,
    slot_ref,
    span_ref,
    loading_grad_ref,
    factor_grad_ref,
    growth,
    table,
    table_t,
    load_own,
    load_wide,
    load_t,
    offset,
    fac_recv,
    fac,
    fac_t,
    total,
    part,
    part_recv,
    local_w,
    span_w,
    span_recv,
    slot_w,
    factor_acc,
    factor_t,
    grad_send,
    grad_recv,
    load_sem,
    fac_ssem,
    fac_rsem,
    part_ssem,
    part_rsem,
    span_ssem,
    span_rsem,
    grad_ssem,
    grad_rsem,
):
    me_path = lax.axis_index("path")
    me_trade = lax.axis_index("trade")
    dates, factor_count, path_local = factors_ref.shape
    dates_own = dates // n_path
    dates_out = dates // n_trade
    groups = dates_own // dates_out
    trades = loadings_ref.shape[2]
    spans = loss_span_ref.shape[1]
    span_slots = span_ref.shape[1]
    locals_ = loss_local_ref.shape[1]
    slots = span_slots + locals_
    path_total = n_path * path_local
    steps = trades // chunk
    first_date = me_path * dates_own

    def path_at(step):
        return lax.rem(me_path + step + n_path, n_path)

    def trade_at(step):
        return lax.rem(me_trade + step + n_trade, n_trade)

    def columns(c):
        return pl.ds(pl.multiple_of(c * chunk, chunk), chunk)

    load = pltpu.make_async_copy(
        loadings_ref.at[pl.ds(first_date, dates_own)], load_own, load_sem
    )
    load.start()

    barrier = pltpu.get_barrier_semaphore()
    for a in range(n_path):
        for b in range(n_trade):
            if a or b:
                pl.semaphore_signal(
                    barrier,
                    inc=1,
                    device_id={"path": path_at(a), "trade": trade_at(b)},
                    device_id_type=MESH,
                )
    pl.semaphore_wait(barrier, n_path * n_trade - 1)

    def fac_copy(o):
        there = path_at(o)
        return pltpu.make_async_remote_copy(
            src_ref=factors_ref.at[pl.ds(there * dates_own, dates_own)],
            dst_ref=fac_recv.at[o - 1],
            send_sem=fac_ssem,
            recv_sem=fac_rsem,
            device_id={"path": there},
            device_id_type=MESH,
        )

    for o in range(1, n_path):
        fac_copy(o).start()

    set_match = (
        lax.broadcasted_iota(jnp.int32, (spans, span_slots), 0) == span_ref[...]
    ).astype(f32).astype(bf16)

    @pl.loop(0, steps)
    def _(c):
        cols = columns(c)
        hot = (
            lax.broadcasted_iota(jnp.int32, (slots, chunk), 0) == slot_ref[:, cols]
        ).astype(f32)
        span_hot = dot(set_match, hot[:span_slots].astype(bf16))
        both = jnp.concatenate([span_hot, hot[span_slots:]], axis=0)
        table_t[:, cols] = both.astype(bf16)
        table[cols, :] = both.T.astype(bf16)

    offset[...] = notional_ref[...] * strike_ref[...]
    load.wait()

    for d in range(dates_own):
        row = load_own[d]
        load_wide[d] = jnp.concatenate([row, row, row, row], axis=0)

    @pl.loop(0, steps)
    def _(c):
        cols = columns(c)
        rows = [load_own[d, :, cols].astype(f32) for d in range(dates_own)]
        load_t[cols, :] = jnp.concatenate(rows, axis=0).T.astype(bf16)

    if n_path > 1:
        pltpu.make_async_copy(fac_recv, fac_recv, fac_rsem).wait()

    for d in range(dates_own):
        blocks = [factors_ref[first_date + d]]
        blocks += [fac_recv[o - 1, d] for o in range(1, n_path)]
        whole = jnp.concatenate(blocks, axis=1)
        fac[d] = whole
        scaled = whole.astype(f32) * f32(math.log2(math.e))
        high = scaled.astype(bf16).astype(f32)
        middle = (scaled - high).astype(bf16).astype(f32)
        low = scaled - high - middle
        split = jnp.concatenate([high, middle, low, jnp.zeros_like(low)], axis=0)
        fac_t[d] = split.T.astype(bf16)

    def part_copy(d, o):
        there = trade_at(o)
        return pltpu.make_async_remote_copy(
            src_ref=part.at[d, there],
            dst_ref=part_recv.at[d, o - 1],
            send_sem=part_ssem.at[d],
            recv_sem=part_rsem.at[d],
            device_id={"trade": there},
            device_id_type=MESH,
        )

    def span_copy(d, o):
        return pltpu.make_async_remote_copy(
            src_ref=span_w.at[d],
            dst_ref=span_recv.at[d, o - 1],
            send_sem=span_ssem.at[d],
            recv_sem=span_rsem.at[d],
            device_id={"trade": trade_at(o)},
            device_id_type=MESH,
        )

    def wait_all(buffer, sem):
        pltpu.make_async_copy(buffer, buffer, sem).wait()

    def finish_span(d):
        wait_all(part_recv.at[d], part_rsem.at[d])
        sums = part[d, me_trade]
        for o in range(1, n_trade):
            sums = sums + part_recv[d, o - 1]
        weight = date_weight_ref[first_date + d]
        span_w[d] = (
            weight * loss_span_ref[...] * jax.nn.sigmoid(sums / smoothing)
        ).astype(bf16)
        for o in range(1, n_trade):
            span_copy(d, o).start()

    @pl.loop(0, dates_own)
    def _(d):
        total[...] = jnp.zeros_like(total)

        @pl.loop(0, steps)
        def _(c):
            cols = columns(c)
            exponent = dot(fac_t[d], load_wide[d, :, cols])
            grown = jnp.exp2(exponent) * notional_ref[:, cols]
            growth[d * steps + c] = grown.astype(bf16)
            values = (grown - offset[:, cols]).astype(bf16)
            total[...] += dot(values, table[cols, :])

        part[d] = total[:, :spans].reshape(part.shape[1:])
        for o in range(1, n_trade):
            part_copy(d, o).start()
        weight = date_weight_ref[first_date + d]
        local_w[d] = (
            weight * loss_local_ref[...] * jax.nn.sigmoid(total[:, spans:] / smoothing)
        ).astype(bf16)

        @pl.when(d > 0)
        def _():
            finish_span(d - 1)

    if dates_own == 1:
        finish_span(0)

    def grad_copy(g, o):
        return pltpu.make_async_remote_copy(
            src_ref=grad_send.at[g, o],
            dst_ref=grad_recv.at[me_trade],
            send_sem=grad_ssem.at[g, o],
            recv_sem=grad_rsem.at[me_trade],
            device_id={"path": path_at(-o), "trade": me_path * groups + g},
            device_id_type=MESH,
        )

    rows = path_total // n_trade

    @pl.loop(0, dates_own)
    def _(d):
        wait_all(span_recv.at[d], span_rsem.at[d])
        slot_w[pl.ds(pl.multiple_of(me_trade * rows, rows), rows), :spans] = span_w[d]
        for o in range(1, n_trade):
            start = pl.multiple_of(trade_at(-o) * rows, rows)
            slot_w[pl.ds(start, rows), :spans] = span_recv[d, o - 1]
        slot_w[:, spans:] = local_w[d]
        factor_acc[...] = jnp.zeros_like(factor_acc)

        @pl.loop(0, steps)
        def _(c):
            cols = columns(c)
            weight = dot(slot_w[...], table_t[:, cols]).astype(bf16)
            sensitivity = weight * growth[d * steps + c]
            loading_grad_ref[d, :, cols] = dot(fac[d], sensitivity) / path_total
            factor_acc[...] += dot(sensitivity, load_t[cols, :])

        factor_t[...] = factor_acc[...].T
        mine = factor_t[pl.ds(pl.multiple_of(d * factor_count, factor_count), factor_count), :]
        g = d // dates_out
        for o in range(n_path):
            grad_send[g, o, lax.rem(d, dates_out)] = mine[
                :, o * path_local : (o + 1) * path_local
            ]

        if dates_own > 1:

            @pl.when(d == 0)
            def _():
                finish_span(dates_own - 1)

        @pl.when(lax.rem(d, dates_out) == dates_out - 1)
        def _():
            here = me_path * groups + g == me_trade

            @pl.when(here)
            def _():
                pltpu.make_async_copy(
                    grad_send.at[g, 0], grad_recv.at[me_trade], grad_rsem.at[me_trade]
                ).start()

            @pl.when(jnp.logical_not(here))
            def _():
                grad_copy(g, 0).start()

            for o in range(1, n_path):
                grad_copy(g, o).start()

    if n_path > 1:
        wait_all(fac_recv, fac_ssem)
    for d in range(dates_own):
        wait_all(part_recv.at[d], part_ssem.at[d])
        wait_all(span_recv.at[d], span_ssem.at[d])
    for g in range(groups):

        @pl.when(me_path * groups + g != me_trade)
        def _():
            grad_copy(g, 0).wait_send()

        for o in range(1, n_path):
            grad_copy(g, o).wait_send()

    for b in range(n_trade):
        wait_all(grad_recv.at[b], grad_rsem.at[b])
    sums = grad_recv[0]
    for b in range(1, n_trade):
        sums = sums + grad_recv[b]
    factor_grad_ref[...] = sums


def on_device(
    n_path,
    n_trade,
    factors,
    loadings,
    notional,
    strike,
    date_weight,
    loss_spanning,
    loss_local,
    trade_slot,
    span_list,
):
    dates, factor_count, path_local = factors.shape
    trades = loadings.shape[2]
    spans = loss_spanning.shape[0]
    locals_ = loss_local.shape[0]
    width = spans + locals_
    paths = n_path * path_local
    rows = paths // n_trade
    dates_own = dates // n_path
    dates_out = dates // n_trade
    groups = dates_own // dates_out
    vmem = pl.BlockSpec(memory_space=pltpu.VMEM)
    dma = pltpu.SemaphoreType.DMA
    return pl.pallas_call(
        functools.partial(kernel, n_path, n_trade),
        out_shape=(
            jax.ShapeDtypeStruct((dates_own, factor_count, trades), f32),
            jax.ShapeDtypeStruct((dates_out, factor_count, path_local), f32),
        ),
        in_specs=[
            vmem,
            pl.BlockSpec(memory_space=pl.ANY),
            vmem,
            vmem,
            pl.BlockSpec(memory_space=pltpu.SMEM),
            vmem,
            vmem,
            vmem,
            vmem,
        ],
        out_specs=(vmem, vmem),
        scratch_shapes=[
            pltpu.VMEM((dates_own * (trades // chunk), paths, chunk), bf16),
            pltpu.VMEM((trades, width), bf16),
            pltpu.VMEM((width, trades), bf16),
            pltpu.VMEM((dates_own, factor_count, trades), bf16),
            pltpu.VMEM((dates_own, 4 * factor_count, trades), bf16),
            pltpu.VMEM((trades, dates_own * factor_count), bf16),
            pltpu.VMEM((1, trades), f32),
            pltpu.VMEM((max(n_path - 1, 1), dates_own, factor_count, path_local), bf16),
            pltpu.VMEM((dates_own, factor_count, paths), bf16),
            pltpu.VMEM((dates_own, paths, 4 * factor_count), bf16),
            pltpu.VMEM((paths, width), f32),
            pltpu.VMEM((dates_own, n_trade, rows, spans), f32),
            pltpu.VMEM((dates_own, n_trade - 1, rows, spans), f32),
            pltpu.VMEM((dates_own, paths, locals_), bf16),
            pltpu.VMEM((dates_own, rows, spans), bf16),
            pltpu.VMEM((dates_own, n_trade - 1, rows, spans), bf16),
            pltpu.VMEM((paths, width), bf16),
            pltpu.VMEM((paths, dates_own * factor_count), f32),
            pltpu.VMEM((dates_own * factor_count, paths), f32),
            pltpu.VMEM((groups, n_path, dates_out, factor_count, path_local), f32),
            pltpu.VMEM((n_trade, dates_out, factor_count, path_local), f32),
            dma,
            dma,
            dma,
            dma((dates_own,)),
            dma((dates_own,)),
            dma((dates_own,)),
            dma((dates_own,)),
            dma((groups, n_path)),
            dma((n_trade,)),
        ],
        compiler_params=pltpu.CompilerParams(
            collective_id=0, has_side_effects=True, vmem_limit_bytes=67043328
        ),
    )(
        factors,
        loadings,
        notional[None],
        strike[None],
        date_weight,
        loss_spanning[None],
        loss_local[None],
        trade_slot[None],
        span_list[None],
    )


def solution(mesh):
    return jax.shard_map(
        functools.partial(on_device, mesh.shape["path"], mesh.shape["trade"]),
        mesh=mesh,
        in_specs=(
            P(None, None, "path"),
            P(None, None, "trade"),
            P("trade"),
            P("trade"),
            P(),
            P(),
            P("trade"),
            P("trade"),
            P("trade"),
        ),
        out_specs=(P("path", None, "trade"), P("trade", None, "path")),
        check_vma=False,
    )
```

time: 287 us -> 92.5 us (0.32); the launches traced: 282 us -> 92.3 us
  matrix products: 110 us -> 0 us
  waiting for transfers between devices: 93.3 us -> 0 us
  Pallas kernels: 0 us -> 88.7 us
  local copies, waits for them, and re-layouts: 33.8 us -> 2.88 us
  other arithmetic: 15.8 us -> 0 us
  between operations: 14.1 us -> 0.65 us
  blocking collectives: 8.99 us -> 0 us
  starting transfers between devices: 4.78 us -> 0 us
    dot_general x56 -> x0, matrix products: 110 us -> none  [the longest x8 26.4 us: forward(): jnp.einsum('bpk,ks->bps', values, slot_table, preferred_element_type=jnp....]
    pallas_call x0 -> x1, Pallas kernels: none -> 88.7 us  [on_device(): pl.pallas_call(functools.partial(kernel, n_path, n_trade), out_shape=(jax...]
    psum x1 -> x0, waiting for transfers between devices: 59 us -> none  [on_device(): span_total = lax.psum(span_parts, 'trade')]
    reduce_scatter x1 -> x0, waiting for transfers between devices: 30.5 us -> none  [on_device(): lax.psum_scatter(regrouped, 'trade', scatter_dimension=0, tiled=True)]
    dynamic_slice x25 -> x0, local copies, waits for them, and re-layouts: 12.8 us -> none  [the longest x16 8.27 us: on_device(): lax.map(adjoint, (factor_blocks, loading_blocks, span_blocks, local_weigh...]
    all_to_all x1 -> x0, blocking collectives: 8.99 us -> none  [on_device(): lax.all_to_all(factor_terms, 'path', split_axis=2, concat_axis=0, tiled=T...]
    while x81 -> x0, local copies, waits for them, and re-layouts: 8.04 us -> none
    unnamed x15 -> x4, local copies, waits for them, and re-layouts: 8.86 us -> 2.88 us
  transfers between devices with their start and end apart: 3 -> 0, of which waited for: 3 -> 0; matrix products, arithmetic and copies ran while one was open for 1% -> 0% of each run, Pallas kernels for 0% -> 0%
where the time goes in v1:
time: 92.5 us; the launch traced here: 92.3 us
  Pallas kernels  88.7 us (96%)
  local copies, waits for them, and re-layouts  2.88 us (3%)
    pallas_call x1, Pallas kernels, on_device(): pl.pallas_call(functools.partial(kernel, n_path, n_trade), out_shape=(jax...  88.7 us
    unnamed x4, local copies, waits for them, and re-layouts  2.88 us

profile of v1, /device:TPU:7, one launch (start us, length us, event | category | flops | bytes accessed | tf_op | source)
XLA Modules:
  0.0 92.3 jit_solution(16063042772976489352)
XLA Ops:
  0.6 88.7 %shard_map.104 = (f32[8,8,4096]{2,1,0:T(8,128)}, f32[4,8,128]{2,1,0:T(8,128)}) custom-call(bf16[32,8,128]{2,1,0:T(8,128)(2,1)} %factors_ref.1, bf16[32,8,4096]{2,1,0:T(8,128)(2,1)} %loadings_ref.1, f32[1,4096]{1,0:T(1,128)} %bitcast.6, f32[1,4096]{1,0:T(1,128)} %bitcast.7, f32[32]{0:T(128)} %date_weight_ref.1, f32[1,128]{1,0:T(1,128)} %bitcast.9, ...), custom_call_target="tpu_custom_call" | custom-call | tf_op jit(solution)/shard_map/pallas_call | solution.py:337
  89.4 0.0 copy-start
  89.4 2.3 %copy.13 = f32[8,8,4096]{2,1,0:T(8,128)} copy(f32[8,8,4096]{2,1,0:T(8,128)} %get-tuple-element.4) | data formatting | bytes 2097152
  91.7 0.0 copy-done
  91.7 0.6 copy.14
Async XLA Ops:
  89.4 2.3 %copy-start = (f32[4,8,128]{2,1,0:T(8,128)S(1)}, f32[4,8,128]{2,1,0:T(8,128)}, u32[]{:S(2)}) copy-start(f32[4,8,128]{2,1,0:T(8,128)} %get-tuple-element.5) | copy-start | bytes 49156

commit v2 on v1

--- a/solution.py
+++ b/solution.py
@@ -10,9 +10,12 @@
 
 smoothing = 0.5
 MESH = pl.DeviceIdType.MESH
-chunk = 512
 bf16 = jnp.bfloat16
 f32 = jnp.float32
+
+
+def chunk_of(paths, trades):
+    return math.gcd(trades, (1 << 20) // paths)
 
 
 def dot(a, b):
@@ -45,10 +48,12 @@
     fac_t,
     total,
     part,
-    part_recv,
+    pair_recv,
+    chip_sum,
+    cross_recv,
     local_w,
-    span_w,
-    span_recv,
+    span_half,
+    span_other,
     slot_w,
     factor_acc,
     factor_t,
@@ -57,10 +62,14 @@
     load_sem,
     fac_ssem,
     fac_rsem,
-    part_ssem,
-    part_rsem,
-    span_ssem,
-    span_rsem,
+    pair_ssem,
+    pair_rsem,
+    cross_ssem,
+    cross_rsem,
+    half_ssem,
+    half_rsem,
+    other_ssem,
+    other_rsem,
     grad_ssem,
     grad_rsem,
 ):
@@ -76,14 +85,23 @@
     locals_ = loss_local_ref.shape[1]
     slots = span_slots + locals_
     path_total = n_path * path_local
+    chunk = chunk_of(path_total, trades)
     steps = trades // chunk
     first_date = me_path * dates_own
+    rows = path_total // n_trade
+    chips = n_trade // 2
+    me_chip = me_trade // 2
+    me_core = lax.rem(me_trade, 2)
+    sibling = me_trade + 1 - 2 * me_core
 
     def path_at(step):
         return lax.rem(me_path + step + n_path, n_path)
 
     def trade_at(step):
         return lax.rem(me_trade + step + n_trade, n_trade)
+
+    def chip_at(step):
+        return lax.rem(me_chip + step + chips, chips)
 
     def columns(c):
         return pl.ds(pl.multiple_of(c * chunk, chunk), chunk)
@@ -103,6 +121,21 @@
                     device_id={"path": path_at(a), "trade": trade_at(b)},
                     device_id_type=MESH,
                 )
+    set_match = (
+        lax.broadcasted_iota(jnp.int32, (spans, span_slots), 0) == span_ref[...]
+    ).astype(f32).astype(bf16)
+
+    @pl.loop(0, steps)
+    def _(c):
+        cols = columns(c)
+        hot = (
+            lax.broadcasted_iota(jnp.int32, (slots, chunk), 0) == slot_ref[:, cols]
+        ).astype(f32)
+        span_hot = dot(set_match, hot[:span_slots].astype(bf16))
+        both = jnp.concatenate([span_hot, hot[span_slots:]], axis=0)
+        table_t[:, cols] = both.astype(bf16)
+        table[cols, :] = both.T.astype(bf16)
+
     pl.semaphore_wait(barrier, n_path * n_trade - 1)
 
     def fac_copy(o):
@@ -118,21 +151,6 @@
 
     for o in range(1, n_path):
         fac_copy(o).start()
-
-    set_match = (
-        lax.broadcasted_iota(jnp.int32, (spans, span_slots), 0) == span_ref[...]
-    ).astype(f32).astype(bf16)
-
-    @pl.loop(0, steps)
-    def _(c):
-        cols = columns(c)
-        hot = (
-            lax.broadcasted_iota(jnp.int32, (slots, chunk), 0) == slot_ref[:, cols]
-        ).astype(f32)
-        span_hot = dot(set_match, hot[:span_slots].astype(bf16))
-        both = jnp.concatenate([span_hot, hot[span_slots:]], axis=0)
-        table_t[:, cols] = both.astype(bf16)
-        table[cols, :] = both.T.astype(bf16)
 
     offset[...] = notional_ref[...] * strike_ref[...]
     load.wait()
@@ -162,41 +180,64 @@
         split = jnp.concatenate([high, middle, low, jnp.zeros_like(low)], axis=0)
         fac_t[d] = split.T.astype(bf16)
 
-    def part_copy(d, o):
-        there = trade_at(o)
-        return pltpu.make_async_remote_copy(
-            src_ref=part.at[d, there],
-            dst_ref=part_recv.at[d, o - 1],
-            send_sem=part_ssem.at[d],
-            recv_sem=part_rsem.at[d],
-            device_id={"trade": there},
-            device_id_type=MESH,
-        )
-
-    def span_copy(d, o):
-        return pltpu.make_async_remote_copy(
-            src_ref=span_w.at[d],
-            dst_ref=span_recv.at[d, o - 1],
-            send_sem=span_ssem.at[d],
-            recv_sem=span_rsem.at[d],
-            device_id={"trade": trade_at(o)},
-            device_id_type=MESH,
-        )
-
     def wait_all(buffer, sem):
         pltpu.make_async_copy(buffer, buffer, sem).wait()
 
-    def finish_span(d):
-        wait_all(part_recv.at[d], part_rsem.at[d])
-        sums = part[d, me_trade]
-        for o in range(1, n_trade):
-            sums = sums + part_recv[d, o - 1]
+    def send_pair(d):
+        pltpu.make_async_remote_copy(
+            src_ref=part.at[d, 1 - me_core],
+            dst_ref=pair_recv.at[d],
+            send_sem=pair_ssem.at[d],
+            recv_sem=pair_rsem.at[d],
+            device_id={"trade": sibling},
+            device_id_type=MESH,
+        ).start()
+
+    def send_cross(d):
+        wait_all(pair_recv.at[d], pair_rsem.at[d])
+        chip_sum[d] = part[d, me_core] + pair_recv[d]
+        for o in range(1, chips):
+            there = chip_at(o)
+            pltpu.make_async_remote_copy(
+                src_ref=chip_sum.at[d, there],
+                dst_ref=cross_recv.at[d, o - 1],
+                send_sem=cross_ssem.at[d],
+                recv_sem=cross_rsem.at[d],
+                device_id={"trade": there * 2 + me_core},
+                device_id_type=MESH,
+            ).start()
+
+    def send_half(d):
+        wait_all(cross_recv.at[d], cross_rsem.at[d])
+        sums = chip_sum[d, me_chip]
+        for o in range(1, chips):
+            sums = sums + cross_recv[d, o - 1]
         weight = date_weight_ref[first_date + d]
-        span_w[d] = (
+        span_half[d, 0] = (
             weight * loss_span_ref[...] * jax.nn.sigmoid(sums / smoothing)
         ).astype(bf16)
-        for o in range(1, n_trade):
-            span_copy(d, o).start()
+        for o in range(1, chips):
+            pltpu.make_async_remote_copy(
+                src_ref=span_half.at[d, 0],
+                dst_ref=span_half.at[d, o],
+                send_sem=half_ssem.at[d],
+                recv_sem=half_rsem.at[d],
+                device_id={"trade": chip_at(o) * 2 + me_core},
+                device_id_type=MESH,
+            ).start()
+
+    def send_other(d):
+        wait_all(span_half.at[d, pl.ds(1, chips - 1)], half_rsem.at[d])
+        pltpu.make_async_remote_copy(
+            src_ref=span_half.at[d],
+            dst_ref=span_other.at[d],
+            send_sem=other_ssem.at[d],
+            recv_sem=other_rsem.at[d],
+            device_id={"trade": sibling},
+            device_id_type=MESH,
+        ).start()
+
+    stages = (send_cross, send_half, send_other)
 
     @pl.loop(0, dates_own)
     def _(d):
@@ -211,20 +252,19 @@
             values = (grown - offset[:, cols]).astype(bf16)
             total[...] += dot(values, table[cols, :])
 
-        part[d] = total[:, :spans].reshape(part.shape[1:])
-        for o in range(1, n_trade):
-            part_copy(d, o).start()
+        for r in range(n_trade):
+            part[d, r % 2, r // 2] = total[r * rows : (r + 1) * rows, :spans]
+        send_pair(d)
         weight = date_weight_ref[first_date + d]
         local_w[d] = (
             weight * loss_local_ref[...] * jax.nn.sigmoid(total[:, spans:] / smoothing)
         ).astype(bf16)
 
-        @pl.when(d > 0)
-        def _():
-            finish_span(d - 1)
-
-    if dates_own == 1:
-        finish_span(0)
+        for late, stage in enumerate(stages, 1):
+
+            @pl.when(d >= late)
+            def _(late=late, stage=stage):
+                stage(d - late)
 
     def grad_copy(g, o):
         return pltpu.make_async_remote_copy(
@@ -236,15 +276,13 @@
             device_id_type=MESH,
         )
 
-    rows = path_total // n_trade
-
     @pl.loop(0, dates_own)
     def _(d):
-        wait_all(span_recv.at[d], span_rsem.at[d])
-        slot_w[pl.ds(pl.multiple_of(me_trade * rows, rows), rows), :spans] = span_w[d]
-        for o in range(1, n_trade):
-            start = pl.multiple_of(trade_at(-o) * rows, rows)
-            slot_w[pl.ds(start, rows), :spans] = span_recv[d, o - 1]
+        wait_all(span_other.at[d], other_rsem.at[d])
+        for o in range(chips):
+            for core, source in ((me_core, span_half), (1 - me_core, span_other)):
+                start = pl.multiple_of((chip_at(-o) * 2 + core) * rows, rows)
+                slot_w[pl.ds(start, rows), :spans] = source[d, o]
         slot_w[:, spans:] = local_w[d]
         factor_acc[...] = jnp.zeros_like(factor_acc)
 
@@ -264,11 +302,11 @@
                 :, o * path_local : (o + 1) * path_local
             ]
 
-        if dates_own > 1:
-
-            @pl.when(d == 0)
-            def _():
-                finish_span(dates_own - 1)
+        for late, stage in enumerate(stages, 1):
+
+            @pl.when(d < late)
+            def _(late=late, stage=stage):
+                stage(d + dates_own - late)
 
         @pl.when(lax.rem(d, dates_out) == dates_out - 1)
         def _():
@@ -290,8 +328,10 @@
     if n_path > 1:
         wait_all(fac_recv, fac_ssem)
     for d in range(dates_own):
-        wait_all(part_recv.at[d], part_ssem.at[d])
-        wait_all(span_recv.at[d], span_ssem.at[d])
+        wait_all(pair_recv.at[d], pair_ssem.at[d])
+        wait_all(cross_recv.at[d], cross_ssem.at[d])
+        wait_all(span_half.at[d, pl.ds(1, chips - 1)], half_ssem.at[d])
+        wait_all(span_other.at[d], other_ssem.at[d])
     for g in range(groups):
 
         @pl.when(me_path * groups + g != me_trade)
@@ -329,9 +369,11 @@
     width = spans + locals_
     paths = n_path * path_local
     rows = paths // n_trade
+    chips = n_trade // 2
     dates_own = dates // n_path
     dates_out = dates // n_trade
     groups = dates_own // dates_out
+    chunk = chunk_of(paths, trades)
     vmem = pl.BlockSpec(memory_space=pltpu.VMEM)
     dma = pltpu.SemaphoreType.DMA
     return pl.pallas_call(
@@ -364,11 +406,13 @@
             pltpu.VMEM((dates_own, factor_count, paths), bf16),
             pltpu.VMEM((dates_own, paths, 4 * factor_count), bf16),
             pltpu.VMEM((paths, width), f32),
-            pltpu.VMEM((dates_own, n_trade, rows, spans), f32),
-            pltpu.VMEM((dates_own, n_trade - 1, rows, spans), f32),
+            pltpu.VMEM((dates_own, 2, chips, rows, spans), f32),
+            pltpu.VMEM((dates_own, chips, rows, spans), f32),
+            pltpu.VMEM((dates_own, chips, rows, spans), f32),
+            pltpu.VMEM((dates_own, chips - 1, rows, spans), f32),
             pltpu.VMEM((dates_own, paths, locals_), bf16),
-            pltpu.VMEM((dates_own, rows, spans), bf16),
-            pltpu.VMEM((dates_own, n_trade - 1, rows, spans), bf16),
+            pltpu.VMEM((dates_own, chips, rows, spans), bf16),
+            pltpu.VMEM((dates_own, chips, rows, spans), bf16),
             pltpu.VMEM((paths, width), bf16),
             pltpu.VMEM((paths, dates_own * factor_count), f32),
             pltpu.VMEM((dates_own * factor_count, paths), f32),
@@ -377,6 +421,10 @@
             dma,
             dma,
             dma,
+            dma((dates_own,)),
+            dma((dates_own,)),
+            dma((dates_own,)),
+            dma((dates_own,)),
             dma((dates_own,)),
             dma((dates_own,)),
             dma((dates_own,)),

time: 92.5 us -> 75.5 us (0.82)
  Pallas kernels: 88.7 us -> 71.8 us
    pallas_call x1, Pallas kernels: 88.7 us -> 71.8 us  [on_device(): pl.pallas_call(functools.partial(kernel, n_path, n_trade), out_shape=(jax...]
where the time goes in v2:
time: 75.5 us; the launch traced here: 75.3 us
  Pallas kernels  71.8 us (95%)
  local copies, waits for them, and re-layouts  2.88 us (4%)
    pallas_call x1, Pallas kernels, on_device(): pl.pallas_call(functools.partial(kernel, n_path, n_trade), out_shape=(jax...  71.8 us
    unnamed x4, local copies, waits for them, and re-layouts  2.88 us

profile of v2, /device:TPU:7, one launch (start us, length us, event | category | flops | bytes accessed | tf_op | source)
XLA Modules:
  0.0 75.3 jit_solution(11329191287171223800)
XLA Ops:
  0.6 71.8 %shard_map.104 = (f32[8,8,4096]{2,1,0:T(8,128)}, f32[4,8,128]{2,1,0:T(8,128)}) custom-call(bf16[32,8,128]{2,1,0:T(8,128)(2,1)} %factors_ref.1, bf16[32,8,4096]{2,1,0:T(8,128)(2,1)} %loadings_ref.1, f32[1,4096]{1,0:T(1,128)} %bitcast.6, f32[1,4096]{1,0:T(1,128)} %bitcast.7, f32[32]{0:T(128)} %date_weight_ref.1, f32[1,128]{1,0:T(1,128)} %bitcast.9, ...), custom_call_target="tpu_custom_call" | custom-call | tf_op jit(solution)/shard_map/pallas_call | solution.py:379
  72.4 0.0 copy-start
  72.4 2.3 %copy.13 = f32[8,8,4096]{2,1,0:T(8,128)} copy(f32[8,8,4096]{2,1,0:T(8,128)} %get-tuple-element.4) | data formatting | bytes 2097152
  74.7 0.0 copy-done
  74.7 0.6 copy.14
Async XLA Ops:
  72.4 2.3 %copy-start = (f32[4,8,128]{2,1,0:T(8,128)S(1)}, f32[4,8,128]{2,1,0:T(8,128)}, u32[]{:S(2)}) copy-start(f32[4,8,128]{2,1,0:T(8,128)} %get-tuple-element.5) | copy-start | bytes 49156

commit v3 on v2

--- a/solution.py
+++ b/solution.py
@@ -41,7 +41,6 @@
     table_t,
     load_own,
     load_wide,
-    load_t,
     offset,
     fac_recv,
     fac,
@@ -56,7 +55,6 @@
     span_other,
     slot_w,
     factor_acc,
-    factor_t,
     grad_send,
     grad_recv,
     load_sem,
@@ -159,12 +157,6 @@
         row = load_own[d]
         load_wide[d] = jnp.concatenate([row, row, row, row], axis=0)
 
-    @pl.loop(0, steps)
-    def _(c):
-        cols = columns(c)
-        rows = [load_own[d, :, cols].astype(f32) for d in range(dates_own)]
-        load_t[cols, :] = jnp.concatenate(rows, axis=0).T.astype(bf16)
-
     if n_path > 1:
         pltpu.make_async_copy(fac_recv, fac_recv, fac_rsem).wait()
 
@@ -237,13 +229,14 @@
             device_id_type=MESH,
         ).start()
 
-    stages = (send_cross, send_half, send_other)
+    lag = max(1, (dates_own - 1) // 3)
+    stages = ((lag, send_cross), (2 * lag, send_half), (3 * lag, send_other))
 
     @pl.loop(0, dates_own)
     def _(d):
         total[...] = jnp.zeros_like(total)
 
-        @pl.loop(0, steps)
+        @pl.loop(0, steps, unroll=True)
         def _(c):
             cols = columns(c)
             exponent = dot(fac_t[d], load_wide[d, :, cols])
@@ -260,7 +253,7 @@
             weight * loss_local_ref[...] * jax.nn.sigmoid(total[:, spans:] / smoothing)
         ).astype(bf16)
 
-        for late, stage in enumerate(stages, 1):
+        for late, stage in stages:
 
             @pl.when(d >= late)
             def _(late=late, stage=stage):
@@ -286,23 +279,26 @@
         slot_w[:, spans:] = local_w[d]
         factor_acc[...] = jnp.zeros_like(factor_acc)
 
-        @pl.loop(0, steps)
+        @pl.loop(0, steps, unroll=True)
         def _(c):
             cols = columns(c)
             weight = dot(slot_w[...], table_t[:, cols]).astype(bf16)
             sensitivity = weight * growth[d * steps + c]
             loading_grad_ref[d, :, cols] = dot(fac[d], sensitivity) / path_total
-            factor_acc[...] += dot(sensitivity, load_t[cols, :])
-
-        factor_t[...] = factor_acc[...].T
-        mine = factor_t[pl.ds(pl.multiple_of(d * factor_count, factor_count), factor_count), :]
+            factor_acc[...] += lax.dot_general(
+                load_own[d, :, cols],
+                sensitivity,
+                (((1,), (1,)), ((), ())),
+                preferred_element_type=f32,
+            )
+
         g = d // dates_out
         for o in range(n_path):
-            grad_send[g, o, lax.rem(d, dates_out)] = mine[
+            grad_send[g, o, lax.rem(d, dates_out)] = factor_acc[
                 :, o * path_local : (o + 1) * path_local
             ]
 
-        for late, stage in enumerate(stages, 1):
+        for late, stage in stages:
 
             @pl.when(d < late)
             def _(late=late, stage=stage):
@@ -379,8 +375,8 @@
     return pl.pallas_call(
         functools.partial(kernel, n_path, n_trade),
         out_shape=(
-            jax.ShapeDtypeStruct((dates_own, factor_count, trades), f32),
-            jax.ShapeDtypeStruct((dates_out, factor_count, path_local), f32),
+            pltpu.VMEM((dates_own, factor_count, trades), f32),
+            pltpu.VMEM((dates_out, factor_count, path_local), f32),
         ),
         in_specs=[
             vmem,
@@ -400,7 +396,6 @@
             pltpu.VMEM((width, trades), bf16),
             pltpu.VMEM((dates_own, factor_count, trades), bf16),
             pltpu.VMEM((dates_own, 4 * factor_count, trades), bf16),
-            pltpu.VMEM((trades, dates_own * factor_count), bf16),
             pltpu.VMEM((1, trades), f32),
             pltpu.VMEM((max(n_path - 1, 1), dates_own, factor_count, path_local), bf16),
             pltpu.VMEM((dates_own, factor_count, paths), bf16),
@@ -414,8 +409,7 @@
             pltpu.VMEM((dates_own, chips, rows, spans), bf16),
             pltpu.VMEM((dates_own, chips, rows, spans), bf16),
             pltpu.VMEM((paths, width), bf16),
-            pltpu.VMEM((paths, dates_own * factor_count), f32),
-            pltpu.VMEM((dates_own * factor_count, paths), f32),
+            pltpu.VMEM((factor_count, paths), f32),
             pltpu.VMEM((groups, n_path, dates_out, factor_count, path_local), f32),
             pltpu.VMEM((n_trade, dates_out, factor_count, path_local), f32),
             dma,
@@ -433,7 +427,7 @@
             dma((n_trade,)),
         ],
         compiler_params=pltpu.CompilerParams(
-            collective_id=0, has_side_effects=True, vmem_limit_bytes=67043328
+            collective_id=0, has_side_effects=True, vmem_limit_bytes=61 << 20
         ),
     )(
         factors,

time: 75.5 us -> 62.9 us (0.83)
  Pallas kernels: 71.8 us -> 60.5 us
  local copies, waits for them, and re-layouts: 2.88 us -> 1.58 us
    pallas_call x1, Pallas kernels: 71.8 us -> 60.5 us  [on_device(): pl.pallas_call(functools.partial(kernel, n_path, n_trade), out_shape=(plt...]
    unnamed x4 -> x2, local copies, waits for them, and re-layouts: 2.88 us -> 1.58 us
where the time goes in v3:
time: 62.9 us; the launch traced here: 62.7 us
  Pallas kernels  60.5 us (96%)
  local copies, waits for them, and re-layouts  1.58 us (3%)
  between operations  0.64 us (1%)
    pallas_call x1, Pallas kernels, on_device(): pl.pallas_call(functools.partial(kernel, n_path, n_trade), out_shape=(plt...  60.5 us
    unnamed x2, local copies, waits for them, and re-layouts  1.58 us

profile of v3, /device:TPU:7, one launch (start us, length us, event | category | flops | bytes accessed | tf_op | source)
XLA Modules:
  0.0 62.7 jit_solution(13012519812644449545)
XLA Ops:
  0.6 60.5 %shard_map.104 = (f32[8,8,4096]{2,1,0:T(8,128)S(1)}, f32[4,8,128]{2,1,0:T(8,128)S(1)}) custom-call(bf16[32,8,128]{2,1,0:T(8,128)(2,1)} %factors_ref.1, bf16[32,8,4096]{2,1,0:T(8,128)(2,1)} %loadings_ref.1, f32[1,4096]{1,0:T(1,128)} %bitcast.6, f32[1,4096]{1,0:T(1,128)} %bitcast.7, f32[32]{0:T(128)} %date_weight_ref.1, f32[1,128]{1,0:T(1,128)} %bitcast.9, ...), custom_call_target="tpu_custom_call" | custom-call | tf_op jit(solution)/shard_map/pallas_call | solution.py:375
  61.2 1.0 %copy.13 = f32[8,8,4096]{2,1,0:T(8,128)} copy(f32[8,8,4096]{2,1,0:T(8,128)S(1)} %get-tuple-element.2) | data formatting | bytes 2097152
  62.1 0.6 copy.14
